TPU v7x, 256 devices: a whole 4x4x8 slice. The times are simulated.
256 devices in a mesh: wide: 32 (over z_hi, y, x), narrow: 8 (over z_lo, core).
Axes of the slice: x: 4, y: 4, z: 8 (z_hi: 2, z_lo: 4; z = z_hi * 4 + z_lo), core: 2. Of those that a mesh axis runs over, the one named last changes fastest.
Arguments:
- tile_pool: bfloat16 [32, 1024, 768], P('wide', 'narrow'), may hold values from -96 to 96
- batch_index: int32 [32, 2048], P('wide', 'narrow'), may hold values from 0 to 127
- pair_label: int32 [32, 2048], P('wide', 'narrow'), may hold values from 0 to 255, as said below
- w_first: bfloat16 [768, 2048], P('narrow'), may hold values from -0.375 to 0.375
- w_second: bfloat16 [2048, 2048], P('narrow'), may hold values from -0.375 to 0.375
- m_first: bfloat16 [32, 768, 2048], P('wide', 'narrow'), may hold values from -0.01275776 to 0.01275776
- m_second: bfloat16 [32, 2048, 2048], P('wide', 'narrow'), may hold values from -0.0078125 to 0.0078125
- v_first: bfloat16 [32, 768, 2048], P('wide', 'narrow'), may hold values from 0.0005086263 to 0.025431315
- v_second: bfloat16 [32, 2048, 2048], P('wide', 'narrow'), may hold values from 0.00019073486 to 0.009536743
- mom_first: bfloat16 [768, 2048], P('narrow'), may hold values from -0.1796875 to 0.1796875
- mom_second: bfloat16 [2048, 2048], P('narrow'), may hold values from -0.1796875 to 0.1796875
Outputs:
- new_first: bfloat16 [768, 2048], P('narrow')
- new_second: bfloat16 [2048, 2048], P('narrow')
- mom_out_first: bfloat16 [768, 2048], P('narrow')
- mom_out_second: bfloat16 [2048, 2048], P('narrow')
Inputs may be any that keep to these rules, and one draw needn't show every extreme that they name: `batch_index`: indices count within the pool of the same site and shard. `pair_label`: each row's partner is another row of the same site and shard, counted within that shard's 256 rows, and names the row back.
All inputs are finite; a program needn't handle non-finite values.
Results may differ from a plain program's by a relative error of at most 0.0075.
Values may be sent and summed in bfloat16 or wider, within the bound.
A program may use at most 128 MiB of HBM per device.

v0:
```python
import math
import jax
import jax.numpy as jnp
import numpy as np
from jax import lax
from jax.sharding import Mesh
from jax.sharding import PartitionSpec as P

PIX = 768
MID = 2048
OUT = 2048
logit_scale = 1.0 / 0.07
rate_inner = 0.2
weight_decay = 0.1
beta_first = 0.9
beta_second = 0.95
adam_eps = 1e-08
rate_outer = 0.7
momentum_coef = 0.9
WIDE = ("zh", "y", "x")
NARROW = ("zl", "c")


def adam_delta(grads, first_moment, second_moment, weights):
    moment_one = beta_first * first_moment.astype(jnp.float32) + (1.0 - beta_first) * grads
    moment_two = (
        beta_second * second_moment.astype(jnp.float32) + (1.0 - beta_second) * grads * grads
    )
    return rate_inner * (
        moment_one / (jnp.sqrt(moment_two) + adam_eps) + weight_decay * weights.astype(jnp.float32)
    )


def outer_update(delta, momentum, weights):
    velocity = momentum_coef * momentum.astype(jnp.float32) + delta
    updated = weights.astype(jnp.float32) - rate_outer * (delta + momentum_coef * velocity)
    return (updated.astype(jnp.bfloat16), velocity.astype(jnp.bfloat16))


def embed_gradient(embedded, partner):
    inverse = lax.rsqrt(jnp.sum(embedded * embedded, axis=1, keepdims=True) + OUT * 1e-06)
    unit_rows = embedded * inverse
    unit_half = unit_rows.astype(jnp.bfloat16)
    scores = logit_scale * jnp.dot(unit_half, unit_half.T, preferred_element_type=jnp.float32)
    positions = jnp.arange(embedded.shape[0], dtype=jnp.int32)
    diagonal = positions[:, None] == positions[None, :]
    scores = jnp.where(diagonal, -1e30, scores)
    highest = jnp.max(scores, axis=1, keepdims=True)
    powers = jnp.exp(scores - highest)
    softmax_rows = powers / jnp.sum(powers, axis=1, keepdims=True)
    target = (partner[:, None] == positions[None, :]).astype(jnp.float32)
    score_grad = softmax_rows - target
    paired = (score_grad + score_grad.T).astype(jnp.bfloat16)
    unit_grad = logit_scale * jnp.dot(paired, unit_half, preferred_element_type=jnp.float32)
    embed_grad = inverse * (
        unit_grad - unit_rows * jnp.sum(unit_rows * unit_grad, axis=1, keepdims=True)
    )
    return embed_grad.astype(jnp.bfloat16)


def plane_sum(delta):
    plane = ("y", "x")
    n_plane = lax.axis_size(plane)
    rows, cols = delta.shape
    got = lax.all_to_all(delta, plane, 1, 0, tiled=True)
    return jnp.sum(got.reshape(n_plane, rows, cols // n_plane), axis=0)


def wide_mean_update(delta, momentum, weights, part=None):
    plane = ("y", "x")
    n_plane = lax.axis_size(plane)
    n_half = lax.axis_size("zh")
    sites = n_plane * n_half
    rows, cols = momentum.shape
    p1 = cols // n_plane
    p2 = p1 // n_half
    part = plane_sum(delta) if part is None else part
    got = lax.all_to_all(part, "zh", 1, 0, tiled=True)
    mean = jnp.sum(got.reshape(n_half, rows, p2), axis=0) / sites
    start = lax.axis_index(plane) * p1 + lax.axis_index("zh") * p2
    mom_piece = lax.dynamic_slice_in_dim(momentum, start, p2, axis=1)
    w_piece = lax.dynamic_slice_in_dim(weights, start, p2, axis=1)
    new_piece, vel_piece = outer_update(mean, mom_piece, w_piece)
    both = jnp.stack([new_piece, vel_piece], axis=0)
    back = lax.all_to_all(
        jnp.broadcast_to(both[None], (n_half,) + both.shape), "zh", 0, 0, tiled=True
    )
    back = back.transpose(1, 2, 0, 3).reshape(2, rows, p1)
    back = lax.all_to_all(
        jnp.broadcast_to(back[None], (n_plane,) + back.shape), plane, 0, 0, tiled=True
    )
    back = back.transpose(1, 2, 0, 3).reshape(2, rows, cols)
    return (back[0], back[1])


def gather_weights(w_first, w_second):
    halves = lax.axis_size("zh")
    h = lax.axis_index("zh")
    shards_n = lax.axis_size(NARROW)
    r1 = w_first.shape[0] // halves
    r2 = w_second.shape[0] // halves
    mine = jnp.concatenate(
        [
            lax.dynamic_slice_in_dim(w_first, h * r1, r1, axis=0),
            lax.dynamic_slice_in_dim(w_second, h * r2, r2, axis=0),
        ],
        axis=0,
    )
    got = lax.all_gather(mine, ("zh",) + NARROW, axis=0, tiled=False)
    got = got.reshape(halves, shards_n, r1 + r2, got.shape[-1])
    return (got[:, :, :r1], got[:, :, r1:])


def split_rows(x, like):
    halves, shards_n, r = like.shape[:3]
    return x.reshape(x.shape[0], shards_n, halves, r)


def shards(
    tile_pool,
    batch_index,
    pair_label,
    w_first,
    w_second,
    m_first,
    m_second,
    v_first,
    v_second,
    mom_first,
    mom_second,
):
    inputs = jnp.take(tile_pool[0], batch_index[0], axis=0)
    partner = pair_label[0]
    scale_one = 1.0 / math.sqrt(PIX)
    scale_two = 1.0 / math.sqrt(MID)
    first_whole, second_whole = gather_weights(w_first, w_second)
    hidden = (
        jnp.einsum(
            "bnhr,hnrc->bc",
            split_rows(inputs, first_whole),
            first_whole,
            preferred_element_type=jnp.float32,
        )
        * scale_one
    )
    active_full, gelu_back = jax.vjp(jax.nn.gelu, hidden)
    active = active_full.astype(jnp.bfloat16)
    embedded = (
        jnp.einsum(
            "bnhr,hnrc->bc",
            split_rows(active, second_whole),
            second_whole,
            preferred_element_type=jnp.float32,
        )
        * scale_two
    )
    embed_half = embed_gradient(embedded, partner)
    grad_second = lax.psum_scatter(
        (scale_two * jnp.dot(active.T, embed_half, preferred_element_type=jnp.float32)).astype(
            jnp.bfloat16
        ),
        NARROW,
        scatter_dimension=0,
        tiled=True,
    ).astype(jnp.float32)
    active_grad = scale_two * jnp.einsum(
        "bc,hnrc->bnhr", embed_half, second_whole, preferred_element_type=jnp.float32
    ).reshape(active.shape)
    hidden_half = gelu_back(active_grad)[0].astype(jnp.bfloat16)
    term_first = (
        scale_one * jnp.dot(inputs.T, hidden_half, preferred_element_type=jnp.float32)
    ).astype(jnp.bfloat16)
    term_first, grad_second = lax.optimization_barrier((term_first, grad_second))
    delta_second = adam_delta(grad_second, m_second[0], v_second[0], w_second)
    part_second = plane_sum(delta_second)
    grad_first = lax.psum_scatter(term_first, NARROW, scatter_dimension=0, tiled=True).astype(
        jnp.float32
    )
    delta_first = adam_delta(grad_first, m_first[0], v_first[0], w_first)
    part_first = plane_sum(delta_first)
    rows_first = w_first.shape[0]
    new_w, vel = wide_mean_update(
        None,
        jnp.concatenate([mom_first, mom_second], axis=0),
        jnp.concatenate([w_first, w_second], axis=0),
        jnp.concatenate([part_first, part_second], axis=0),
    )
    return (new_w[:rows_first], new_w[rows_first:], vel[:rows_first], vel[rows_first:])


def solution(mesh):
    zh, y, x = (2, 4, 4)
    devices = np.asarray(mesh.devices)
    wide, narrow = devices.shape
    sub = Mesh(devices.reshape(zh, y, x, narrow // 2, 2), WIDE + NARROW)
    site = P(WIDE, NARROW, None)
    rows = P(NARROW, None)
    return jax.shard_map(
        shards,
        mesh=sub,
        in_specs=(
            site,
            P(WIDE, NARROW),
            P(WIDE, NARROW),
            rows,
            rows,
            site,
            site,
            site,
            site,
            rows,
            rows,
        ),
        out_specs=(rows, rows, rows, rows),
        check_vma=False,
    )
```

profile of v0, /device:TPU:96, one launch (start us, length us, event | category | flops | bytes accessed | tf_op | source)
XLA Modules:
  0.0 355.6 jit_solution(15545826880929783917)
XLA Ops:
  10.3 1.2 gather_fusion
  11.7 70.6 %all-gather.3.cloned.1.call-done = bf16[2816,2048]{1,0:T(8,128)(2,1)} async-done(((bf16[176,2048]{1,0:T(8,128)(2,1)}), bf16[2816,2048]{1,0:T(8,128)(2,1)}) %all-gather.3.cloned.1.call-update) | async-done | bytes 11534352 | tf_op jit(solution)/shard_map/all_gather | solution.py:109
  82.3 4.8 %multiply_convert_fusion.3 = (bf16[256,2048]{1,0:T(8,128)(2,1)S(1)}, f32[256,2048]{1,0:T(8,128)}) fusion(bf16[2,8,176,2048]{3,2,1,0:T(8,128)(2,1)} %bitcast.96, bf16[256,8,2,48]{0,3,2,1:T(8,128)(2,1)S(1)} %bitcast.93, pred[256]{0:T(512)(128)(4,1)S(1)} %compare_and_fusion), kind=kOutput, calls=%fused_computation.35 | convolution fusion | flops 810745856 | bytes 6684928 | tf_op jit(solution)/shard_map/bnhr,hnrc->bc/dot_general | solution.py:138
  88.1 1.5 reshape.106
  89.7 5.2 %multiply_reduce_fusion.1 = (f32[256]{0:T(256)S(1)}, f32[256,2048]{1,0:T(8,128)S(1)}) fusion(bf16[2,8,176,2048]{3,2,1,0:T(8,128)(2,1)} %bitcast.97, bf16[256,8,2,128]{3,2,1,0:T(2,128)(2,1)} %reshape.106), kind=kOutput, calls=%fused_computation.34 | convolution fusion | flops 2149056256 | bytes 11535360 | tf_op jit(solution)/shard_map/bnhr,hnrc->bc/dot_general | solution.py:149
  98.2 5.7 %multiply_convert_fusion = bf16[2048,2048]{1,0:T(8,128)(2,1)} fusion(bf16[256,2048]{1,0:T(8,128)(2,1)S(1)} %copy-done.7, bf16[256,2048]{1,0:T(8,128)(2,1)S(1)} %multiply_convert_fusion.2), kind=kOutput, calls=%fused_computation.1 | convolution fusion | flops 2155872256 | bytes 10485760 | tf_op jit(solution)/shard_map/dot_general | solution.py:159
  105.1 7.1 %multiply_bitcast_fusion = f32[256,8,2,128]{0,3,1,2:T(8,128)} fusion(bf16[2,8,176,2048]{3,2,1,0:T(8,128)(2,1)} %bitcast.98, bf16[256,2048]{1,0:T(8,128)(2,1)S(1)} %copy-done.9), kind=kOutput, calls=%fused_computation.31 | convolution fusion | flops 2148007936 | bytes 11534336 | tf_op jit(solution)/shard_map/bc,hnrc->bnhr/dot_general | solution.py:166
  112.3 3.4 copy.48
  115.7 2.7 mul.261
  118.3 6.1 %multiply_convert_fusion.1 = bf16[768,2048]{1,0:T(8,128)(2,1)} fusion(f32[256,2048]{1,0:T(8,128)} %get-tuple-element.21, f32[256,2048]{1,0:T(8,128)} %mul.261, bf16[256,768]{1,0:T(8,128)(2,1)S(1)} %gather_fusion, pred[256]{0:T(512)(128)(4,1)S(1)} %compare_and_fusion), kind=kOutput, calls=%fused_computation.6 | convolution fusion | flops 819134464 | bytes 7733504 | tf_op jit(solution)/shard_map/dot_general | solution.py:171
  124.5 70.9 %reduce-scatter.3.cloned.1.call-done = bf16[256,2048]{1,0:T(8,128)(2,1)} async-done(((bf16[2048,2048]{1,0:T(8,128)(2,1)}), bf16[256,2048]{1,0:T(8,128)(2,1)}) %reduce-scatter.3.cloned.1.call-update) | async-done | bytes 1048592 | tf_op jit(solution)/shard_map/reduce_scatter | solution.py:158
  195.4 1.5 convert_element_type.78
  196.9 1.2 copy-done.2
  198.1 4.5 %copy_bitcast_fusion = f32[256,16,128]{2,0,1:T(8,128)} fusion(bf16[256,2048]{1,0:T(8,128)(2,1)S(1)} %copy-done.2, f32[256,2048]{1,0:T(8,128)S(1)} %convert_element_type.78, bf16[1,256,2048]{2,1,0:T(8,128)(2,1)} %param.19, bf16[1,256,2048]{2,1,0:T(8,128)(2,1)} %param.17), kind=kLoop, calls=%fused_computation.29 | loop fusion | flops 7864320 | bytes 7340032 | tf_op jit(solution)/shard_map/all_to_all | solution.py:65
  202.5 6.8 %all-to-all-start.1 = ((f32[256,16,128]{2,0,1:T(8,128)}), f32[256,16,128]{2,0,1:T(8,128)S(1)}, u32[]{:S(2)}, u32[]{:S(2)}) async-start(f32[256,16,128]{2,0,1:T(8,128)} %copy_bitcast_fusion), calls=%async_computation.3 | async-start | bytes 4194304 | tf_op jit(solution)/shard_map/all_to_all | solution.py:65
  209.3 31.8 %reduce-scatter.5.cloned.1.call-done = bf16[96,2048]{1,0:T(8,128)(2,1)} async-done(((bf16[768,2048]{1,0:T(8,128)(2,1)}), bf16[96,2048]{1,0:T(8,128)(2,1)}) %reduce-scatter.5.cloned.1.call-update) | async-done | bytes 393232 | tf_op jit(solution)/shard_map/reduce_scatter | solution.py:176
  241.1 2.8 copy_bitcast_fusion.1
  244.0 6.9 %all-to-all-start = ((f32[96,16,128]{2,0,1:T(8,128)}), f32[96,16,128]{2,0,1:T(8,128)}, u32[]{:S(2)}, u32[]{:S(2)}) async-start(f32[96,16,128]{2,0,1:T(8,128)} %copy_bitcast_fusion.1), calls=%async_computation.2 | async-start | bytes 1572864 | tf_op jit(solution)/shard_map/all_to_all | solution.py:65
  251.0 14.4 %all-to-all-done = f32[96,16,128]{2,0,1:T(8,128)} async-done(((f32[96,16,128]{2,0,1:T(8,128)}), f32[96,16,128]{2,0,1:T(8,128)}, u32[]{:S(2)}, u32[]{:S(2)}) %all-to-all-start) | async-done | bytes 786464 | tf_op jit(solution)/shard_map/all_to_all | solution.py:65
  265.4 1.2 reduce_sum.57
  267.4 5.4 %all-to-all-start.2 = ((f32[352,2,64]{0,2,1:T(8,128)}), f32[352,2,64]{0,2,1:T(8,128)S(1)}, u32[]{:S(2)}, u32[]{:S(2)}) async-start(f32[352,2,64]{0,2,1:T(8,128)} %bitcast.20), calls=%async_computation.4 | async-start | bytes 393216 | tf_op jit(solution)/shard_map/all_to_all | solution.py:78
  273.7 1.5 copy.55
  275.1 2.0 copy.54
  277.1 5.4 %all-to-all-done.2 = f32[352,2,64]{0,2,1:T(8,128)S(1)} async-done(((f32[352,2,64]{0,2,1:T(8,128)}), f32[352,2,64]{0,2,1:T(8,128)S(1)}, u32[]{:S(2)}, u32[]{:S(2)}) %all-to-all-start.2) | async-done | bytes 180256 | tf_op jit(solution)/shard_map/all_to_all | solution.py:78
  283.4 11.3 %all_to_all.49 = bf16[2,2,352,64]{2,3,1,0:T(8,128)(2,1)S(1)} all-to-all(bf16[2,2,352,64]{2,3,1,0:T(8,128)(2,1)S(1)} %broadcast_in_dim.43), channel_id=1, replica_groups=mesh['zh'=2,'y'=4,'x'=4,'zl'=4,'c'=2] {'zh'}, dimensions={0} | all-to-all | bytes 360448 | tf_op jit(solution)/shard_map/all_to_all | solution.py:85
  295.5 39.8 %all_to_all.50 = bf16[16,2,352,128]{3,2,1,0:T(8,128)(2,1)} all-to-all(bf16[16,2,352,128]{3,2,1,0:T(8,128)(2,1)S(1)} %broadcast_in_dim.45), channel_id=1, replica_groups=mesh['zh'=2,'y'=4,'x'=4,'zl'=4,'c'=2] {'y','x'}, dimensions={0} | all-to-all | bytes 5767168 | tf_op jit(solution)/shard_map/all_to_all | solution.py:89
  335.4 3.4 copy.58
  338.8 1.2 fusion.78
  339.9 2.3 fusion.77
  342.3 2.1 copy.66
  344.4 2.3 copy.61
  347.7 1.4 copy.62
  (58 shorter events, 13.1 us)
Async XLA Ops:
  7.2 3.1 copy-start
  7.2 3.1 copy-start.10
  7.2 75.1 %all-gather.3.cloned.1.call-start = ((), (), s32[]{:S(2)}) async-start(), calls=%async_computation.9 | async-start | bytes 12255232 | tf_op jit(solution)/shard_map/all_gather | solution.py:109
  10.2 185.2 %reduce-scatter.3.cloned.1.call-start = ((), (), s32[]{:S(2)}) async-start(), calls=%async_computation.7 | async-start | bytes 9437184 | tf_op jit(solution)/shard_map/reduce_scatter | solution.py:158
  87.2 1.0 copy-start.6
  94.9 1.0 copy-start.11
  96.7 1.5 copy-start.7
  97.3 1.0 copy-start.8
  103.9 1.2 copy-start.9
  103.9 137.2 %reduce-scatter.5.cloned.1.call-start = ((), (), s32[]{:S(2)}) async-start(), calls=%async_computation.8 | async-start | bytes 3538944 | tf_op jit(solution)/shard_map/reduce_scatter | solution.py:176
  196.8 1.2 copy-start.2
  202.5 41.5 %all-to-all-start.1 = ((f32[256,16,128]{2,0,1:T(8,128)}), f32[256,16,128]{2,0,1:T(8,128)S(1)}, u32[]{:S(2)}, u32[]{:S(2)}) async-start(f32[256,16,128]{2,0,1:T(8,128)} %copy_bitcast_fusion), calls=%async_computation.3 | async-start | bytes 4194304 | tf_op jit(solution)/shard_map/all_to_all | solution.py:65
  244.0 21.4 %all-to-all-start = ((f32[96,16,128]{2,0,1:T(8,128)}), f32[96,16,128]{2,0,1:T(8,128)}, u32[]{:S(2)}, u32[]{:S(2)}) async-start(f32[96,16,128]{2,0,1:T(8,128)} %copy_bitcast_fusion.1), calls=%async_computation.2 | async-start | bytes 1572864 | tf_op jit(solution)/shard_map/all_to_all | solution.py:65
  251.0 22.4 %copy-start.4 = (bf16[96,2048]{1,0:T(8,128)(2,1)S(1)}, bf16[96,2048]{1,0:T(8,128)(2,1)}, u32[]{:S(2)}) copy-start(bf16[96,2048]{1,0:T(8,128)(2,1)} %param.14) | copy-start | bytes 1179652
  267.4 15.1 %all-to-all-start.2 = ((f32[352,2,64]{0,2,1:T(8,128)}), f32[352,2,64]{0,2,1:T(8,128)S(1)}, u32[]{:S(2)}, u32[]{:S(2)}) async-start(f32[352,2,64]{0,2,1:T(8,128)} %bitcast.20), calls=%async_computation.4 | async-start | bytes 393216 | tf_op jit(solution)/shard_map/all_to_all | solution.py:78
  342.3 4.4 %copy-start.5 = (bf16[1,96,16,128]{1,3,2,0:T(8,128)(2,1)S(1)}, bf16[1,96,16,128]{1,3,2,0:T(8,128)(2,1)}, u32[]{:S(2)}) copy-start(bf16[1,96,16,128]{1,3,2,0:T(8,128)(2,1)} %get-tuple-element.16) | copy-start | bytes 1179652
  342.3 5.4 %copy-start.3 = (bf16[1,256,16,128]{1,3,2,0:T(8,128)(2,1)S(1)}, bf16[1,256,16,128]{1,3,2,0:T(8,128)(2,1)}, u32[]{:S(2)}) copy-start(bf16[1,256,16,128]{1,3,2,0:T(8,128)(2,1)} %get-tuple-element.14) | copy-start | bytes 3145732
  344.4 4.7 %copy-start.1 = (bf16[1,128,768]{2,1,0:T(8,128)(2,1)S(1)}, bf16[1,128,768]{2,1,0:T(8,128)(2,1)}, u32[]{:S(2)}) copy-start(bf16[1,128,768]{2,1,0:T(8,128)(2,1)} %param.11) | copy-start | bytes 589828
Sparse Core Ops, SparseCore 0:
  10.4 71.8 all-gather.2
  104.1 91.2 reduce-scatter.2
  197.9 43.1 reduce-scatter.4
where the time goes:
time: 357 us; the launch traced here: 356 us
  waiting for transfers between devices  193 us (54%)
  blocking collectives  51.2 us (14%)
  local copies, waits for them, and re-layouts  34.8 us (10%)
  matrix products  30.3 us (8%)
  starting transfers between devices  19.4 us (5%)
  between operations  14.1 us (4%)
  other arithmetic  12.7 us (4%)
    reduce_scatter x1, waiting for transfers between devices, shards(): lax.psum_scatter((scale_two * jnp.dot(active.T, embed_half, preferred_ele...  70.9 us
    all_gather x1, waiting for transfers between devices, gather_weights(): got = lax.all_gather(mine, ('zh',) + NARROW, axis=0, tiled=False)  70.6 us
    all_to_all x1, blocking collectives, wide_mean_update(): lax.all_to_all(jnp.broadcast_to(back[None], (n_plane,) + back.shape), pla...  39.8 us
    reduce_scatter x1, waiting for transfers between devices, shards(): lax.psum_scatter(term_first, NARROW, scatter_dimension=0, tiled=True)  31.8 us
    all_to_all x2, waiting for transfers between devices, plane_sum(): got = lax.all_to_all(delta, plane, 1, 0, tiled=True)  14.4 us
    all_to_all x2, starting transfers between devices, plane_sum(): got = lax.all_to_all(delta, plane, 1, 0, tiled=True)  13.7 us
    unnamed x30, local copies, waits for them, and re-layouts  12.1 us
    all_to_all x1, blocking collectives, wide_mean_update(): lax.all_to_all(jnp.broadcast_to(both[None], (n_half,) + both.shape), 'zh'...  11.3 us
  transfers between devices with their start and end apart: 6, of which 5 were waited for; matrix products, arithmetic and copies ran while one was open for 9% of the time, Pallas kernels for 0%

commit v1 on v0

--- a/solution.py
+++ b/solution.py
@@ -1,3 +1,4 @@
+import functools
 import math
 import jax
 import jax.numpy as jnp
@@ -19,6 +20,21 @@
 momentum_coef = 0.9
 WIDE = ("zh", "y", "x")
 NARROW = ("zl", "c")
+
+
+def set_handle(xin, link_axis, out_dim, where_dim):
+    return jnp.concatenate(
+        jax.lax.all_to_all(
+            jnp.stack(jnp.split(xin, jax.lax.axis_size(link_axis), axis=out_dim)),
+            split_axis=0,
+            concat_axis=0,
+            axis_name=link_axis,
+        ),
+        axis=where_dim,
+    )
+
+
+direct_heads = functools.partial(set_handle, link_axis="zh", out_dim=1, where_dim=0)
 
 
 def adam_delta(grads, first_moment, second_moment, weights):
@@ -75,7 +91,7 @@
     p1 = cols // n_plane
     p2 = p1 // n_half
     part = plane_sum(delta) if part is None else part
-    got = lax.all_to_all(part, "zh", 1, 0, tiled=True)
+    got = direct_heads(part)
     mean = jnp.sum(got.reshape(n_half, rows, p2), axis=0) / sites
     start = lax.axis_index(plane) * p1 + lax.axis_index("zh") * p2
     mom_piece = lax.dynamic_slice_in_dim(momentum, start, p2, axis=1)

time: 357 us -> 357 us (level)
  no operation moved by 1% of the time
where the time goes in v1:
time: 357 us; the launch traced here: 356 us
  waiting for transfers between devices  193 us (54%)
  blocking collectives  51.4 us (14%)
  local copies, waits for them, and re-layouts  34.8 us (10%)
  matrix products  30.3 us (8%)
  starting transfers between devices  19.4 us (5%)
  between operations  14.1 us (4%)
  other arithmetic  12.8 us (4%)
    reduce_scatter x1, waiting for transfers between devices, shards(): lax.psum_scatter((scale_two * jnp.dot(active.T, embed_half, preferred_ele...  70.9 us
    all_gather x1, waiting for transfers between devices, gather_weights(): got = lax.all_gather(mine, ('zh',) + NARROW, axis=0, tiled=False)  70.6 us
    all_to_all x1, blocking collectives, wide_mean_update(): lax.all_to_all(jnp.broadcast_to(back[None], (n_plane,) + back.shape), pla...  40.1 us
    reduce_scatter x1, waiting for transfers between devices, shards(): lax.psum_scatter(term_first, NARROW, scatter_dimension=0, tiled=True)  31.8 us
    all_to_all x2, waiting for transfers between devices, plane_sum(): got = lax.all_to_all(delta, plane, 1, 0, tiled=True)  14.4 us
    all_to_all x2, starting transfers between devices, plane_sum(): got = lax.all_to_all(delta, plane, 1, 0, tiled=True)  13.7 us
    unnamed x30, local copies, waits for them, and re-layouts  12.1 us
    all_to_all x1, blocking collectives, wide_mean_update(): lax.all_to_all(jnp.broadcast_to(both[None], (n_half,) + both.shape), 'zh'...  11.3 us
  transfers between devices with their start and end apart: 6, of which 5 were waited for; matrix products, arithmetic and copies ran while one was open for 9% of the time, Pallas kernels for 0%

profile of v1, /device:TPU:96, one launch (start us, length us, event | category | flops | bytes accessed | tf_op | source)
XLA Modules:
  0.0 355.9 jit_solution(14589145628790348260)
XLA Ops:
  10.3 1.2 gather_fusion
  11.7 70.6 %all-gather.3.cloned.1.call-done = bf16[2816,2048]{1,0:T(8,128)(2,1)} async-done(((bf16[176,2048]{1,0:T(8,128)(2,1)}), bf16[2816,2048]{1,0:T(8,128)(2,1)}) %all-gather.3.cloned.1.call-update) | async-done | bytes 11534352 | tf_op jit(solution)/shard_map/all_gather | solution.py:125
  82.3 4.8 %multiply_convert_fusion.3 = (bf16[256,2048]{1,0:T(8,128)(2,1)S(1)}, f32[256,2048]{1,0:T(8,128)}) fusion(bf16[2,8,176,2048]{3,2,1,0:T(8,128)(2,1)} %bitcast.99, bf16[256,8,2,48]{0,3,2,1:T(8,128)(2,1)S(1)} %bitcast.96, pred[256]{0:T(512)(128)(4,1)S(1)} %compare_and_fusion), kind=kOutput, calls=%fused_computation.35 | convolution fusion | flops 810745856 | bytes 6684928 | tf_op jit(solution)/shard_map/bnhr,hnrc->bc/dot_general | solution.py:154
  88.1 1.5 reshape.101
  89.7 5.2 %multiply_reduce_fusion.1 = (f32[256]{0:T(256)S(1)}, f32[256,2048]{1,0:T(8,128)S(1)}) fusion(bf16[2,8,176,2048]{3,2,1,0:T(8,128)(2,1)} %bitcast.100, bf16[256,8,2,128]{3,2,1,0:T(2,128)(2,1)} %reshape.101), kind=kOutput, calls=%fused_computation.34 | convolution fusion | flops 2149056256 | bytes 11535360 | tf_op jit(solution)/shard_map/bnhr,hnrc->bc/dot_general | solution.py:165
  98.2 5.7 %multiply_convert_fusion = bf16[2048,2048]{1,0:T(8,128)(2,1)} fusion(bf16[256,2048]{1,0:T(8,128)(2,1)S(1)} %copy-done.7, bf16[256,2048]{1,0:T(8,128)(2,1)S(1)} %multiply_convert_fusion.2), kind=kOutput, calls=%fused_computation.1 | convolution fusion | flops 2155872256 | bytes 10485760 | tf_op jit(solution)/shard_map/dot_general | solution.py:175
  105.1 7.1 %multiply_bitcast_fusion = f32[256,8,2,128]{0,3,1,2:T(8,128)} fusion(bf16[2,8,176,2048]{3,2,1,0:T(8,128)(2,1)} %bitcast.101, bf16[256,2048]{1,0:T(8,128)(2,1)S(1)} %copy-done.9), kind=kOutput, calls=%fused_computation.31 | convolution fusion | flops 2148007936 | bytes 11534336 | tf_op jit(solution)/shard_map/bc,hnrc->bnhr/dot_general | solution.py:182
  112.2 3.4 copy.57
  115.6 2.7 mul.261
  118.3 6.1 %multiply_convert_fusion.1 = bf16[768,2048]{1,0:T(8,128)(2,1)} fusion(f32[256,2048]{1,0:T(8,128)} %get-tuple-element.27, f32[256,2048]{1,0:T(8,128)} %mul.261, bf16[256,768]{1,0:T(8,128)(2,1)S(1)} %gather_fusion, pred[256]{0:T(512)(128)(4,1)S(1)} %compare_and_fusion), kind=kOutput, calls=%fused_computation.6 | convolution fusion | flops 819134464 | bytes 7733504 | tf_op jit(solution)/shard_map/dot_general | solution.py:187
  124.4 70.9 %reduce-scatter.3.cloned.1.call-done = bf16[256,2048]{1,0:T(8,128)(2,1)} async-done(((bf16[2048,2048]{1,0:T(8,128)(2,1)}), bf16[256,2048]{1,0:T(8,128)(2,1)}) %reduce-scatter.3.cloned.1.call-update) | async-done | bytes 1048592 | tf_op jit(solution)/shard_map/reduce_scatter | solution.py:174
  195.4 1.5 convert_element_type.78
  196.9 1.2 copy-done.2
  198.1 4.4 %copy_bitcast_fusion = f32[256,16,128]{2,0,1:T(8,128)} fusion(bf16[256,2048]{1,0:T(8,128)(2,1)S(1)} %copy-done.2, f32[256,2048]{1,0:T(8,128)S(1)} %convert_element_type.78, bf16[1,256,2048]{2,1,0:T(8,128)(2,1)} %param.19, bf16[1,256,2048]{2,1,0:T(8,128)(2,1)} %param.17), kind=kLoop, calls=%fused_computation.29 | loop fusion | flops 7864320 | bytes 7340032 | tf_op jit(solution)/shard_map/all_to_all | solution.py:81
  202.5 6.8 %all-to-all-start.1 = ((f32[256,16,128]{2,0,1:T(8,128)}), f32[256,16,128]{2,0,1:T(8,128)S(1)}, u32[]{:S(2)}, u32[]{:S(2)}) async-start(f32[256,16,128]{2,0,1:T(8,128)} %copy_bitcast_fusion), calls=%async_computation.3 | async-start | bytes 4194304 | tf_op jit(solution)/shard_map/all_to_all | solution.py:81
  209.3 31.8 %reduce-scatter.5.cloned.1.call-done = bf16[96,2048]{1,0:T(8,128)(2,1)} async-done(((bf16[768,2048]{1,0:T(8,128)(2,1)}), bf16[96,2048]{1,0:T(8,128)(2,1)}) %reduce-scatter.5.cloned.1.call-update) | async-done | bytes 393232 | tf_op jit(solution)/shard_map/reduce_scatter | solution.py:192
  241.2 2.8 copy_bitcast_fusion.1
  244.0 6.8 %all-to-all-start = ((f32[96,16,128]{2,0,1:T(8,128)}), f32[96,16,128]{2,0,1:T(8,128)}, u32[]{:S(2)}, u32[]{:S(2)}) async-start(f32[96,16,128]{2,0,1:T(8,128)} %copy_bitcast_fusion.1), calls=%async_computation.2 | async-start | bytes 1572864 | tf_op jit(solution)/shard_map/all_to_all | solution.py:81
  251.0 14.4 %all-to-all-done = f32[96,16,128]{2,0,1:T(8,128)} async-done(((f32[96,16,128]{2,0,1:T(8,128)}), f32[96,16,128]{2,0,1:T(8,128)}, u32[]{:S(2)}, u32[]{:S(2)}) %all-to-all-start) | async-done | bytes 786464 | tf_op jit(solution)/shard_map/all_to_all | solution.py:81
  265.4 1.2 reduce_sum.57
  267.6 5.4 %all-to-all-start.2 = ((f32[2,352,64]{1,2,0:T(8,128)}), f32[2,352,64]{1,2,0:T(8,128)S(1)}, u32[]{:S(2)}, u32[]{:S(2)}) async-start(f32[2,352,64]{1,2,0:T(8,128)} %copy.60), calls=%async_computation.4 | async-start | bytes 393216 | tf_op jit(solution)/shard_map/all_to_all | solution.py:27
  273.8 1.5 copy.62
  275.3 2.0 copy.61
  277.3 5.3 %all-to-all-done.2 = f32[2,352,64]{1,2,0:T(8,128)S(1)} async-done(((f32[2,352,64]{1,2,0:T(8,128)}), f32[2,352,64]{1,2,0:T(8,128)S(1)}, u32[]{:S(2)}, u32[]{:S(2)}) %all-to-all-start.2) | async-done | bytes 180256 | tf_op jit(solution)/shard_map/all_to_all | solution.py:27
  283.5 11.3 %all_to_all.41 = bf16[2,2,352,64]{2,3,1,0:T(8,128)(2,1)S(1)} all-to-all(bf16[2,2,352,64]{2,3,1,0:T(8,128)(2,1)S(1)} %broadcast_in_dim.43), channel_id=1, replica_groups=mesh['zh'=2,'y'=4,'x'=4,'zl'=4,'c'=2] {'zh'}, dimensions={0} | all-to-all | bytes 360448 | tf_op jit(solution)/shard_map/all_to_all | solution.py:101
  295.6 40.1 %all_to_all.42 = bf16[16,2,352,128]{3,2,1,0:T(8,128)(2,1)} all-to-all(bf16[16,2,352,128]{3,2,1,0:T(8,128)(2,1)S(1)} %broadcast_in_dim.45), channel_id=1, replica_groups=mesh['zh'=2,'y'=4,'x'=4,'zl'=4,'c'=2] {'y','x'}, dimensions={0} | all-to-all | bytes 5767168 | tf_op jit(solution)/shard_map/all_to_all | solution.py:105
  335.7 3.4 copy.65
  339.1 1.2 fusion.79
  340.3 2.3 fusion.78
  342.6 2.1 copy.73
  344.7 2.3 copy.68
  348.0 1.4 copy.69
  (59 shorter events, 13.2 us)
Async XLA Ops:
  7.2 3.1 copy-start
  7.2 3.1 copy-start.10
  7.2 75.1 %all-gather.3.cloned.1.call-start = ((), (), s32[]{:S(2)}) async-start(), calls=%async_computation.9 | async-start | bytes 12255232 | tf_op jit(solution)/shard_map/all_gather | solution.py:125
  10.2 185.2 %reduce-scatter.3.cloned.1.call-start = ((), (), s32[]{:S(2)}) async-start(), calls=%async_computation.7 | async-start | bytes 9437184 | tf_op jit(solution)/shard_map/reduce_scatter | solution.py:174
  87.2 1.0 copy-start.6
  94.9 1.0 copy-start.11
  96.7 1.5 copy-start.7
  97.3 1.0 copy-start.8
  103.9 1.2 copy-start.9
  103.9 137.2 %reduce-scatter.5.cloned.1.call-start = ((), (), s32[]{:S(2)}) async-start(), calls=%async_computation.8 | async-start | bytes 3538944 | tf_op jit(solution)/shard_map/reduce_scatter | solution.py:192
  196.8 1.2 copy-start.2
  202.5 41.5 %all-to-all-start.1 = ((f32[256,16,128]{2,0,1:T(8,128)}), f32[256,16,128]{2,0,1:T(8,128)S(1)}, u32[]{:S(2)}, u32[]{:S(2)}) async-start(f32[256,16,128]{2,0,1:T(8,128)} %copy_bitcast_fusion), calls=%async_computation.3 | async-start | bytes 4194304 | tf_op jit(solution)/shard_map/all_to_all | solution.py:81
  244.0 21.4 %all-to-all-start = ((f32[96,16,128]{2,0,1:T(8,128)}), f32[96,16,128]{2,0,1:T(8,128)}, u32[]{:S(2)}, u32[]{:S(2)}) async-start(f32[96,16,128]{2,0,1:T(8,128)} %copy_bitcast_fusion.1), calls=%async_computation.2 | async-start | bytes 1572864 | tf_op jit(solution)/shard_map/all_to_all | solution.py:81
  266.6 6.9 %copy-start.4 = (bf16[96,2048]{1,0:T(8,128)(2,1)S(1)}, bf16[96,2048]{1,0:T(8,128)(2,1)}, u32[]{:S(2)}) copy-start(bf16[96,2048]{1,0:T(8,128)(2,1)} %param.14) | copy-start | bytes 1179652
  267.6 15.0 %all-to-all-start.2 = ((f32[2,352,64]{1,2,0:T(8,128)}), f32[2,352,64]{1,2,0:T(8,128)S(1)}, u32[]{:S(2)}, u32[]{:S(2)}) async-start(f32[2,352,64]{1,2,0:T(8,128)} %copy.60), calls=%async_computation.4 | async-start | bytes 393216 | tf_op jit(solution)/shard_map/all_to_all | solution.py:27
  342.6 4.4 %copy-start.5 = (bf16[1,96,16,128]{1,3,2,0:T(8,128)(2,1)S(1)}, bf16[1,96,16,128]{1,3,2,0:T(8,128)(2,1)}, u32[]{:S(2)}) copy-start(bf16[1,96,16,128]{1,3,2,0:T(8,128)(2,1)} %get-tuple-element.20) | copy-start | bytes 1179652
  342.6 5.4 %copy-start.3 = (bf16[1,256,16,128]{1,3,2,0:T(8,128)(2,1)S(1)}, bf16[1,256,16,128]{1,3,2,0:T(8,128)(2,1)}, u32[]{:S(2)}) copy-start(bf16[1,256,16,128]{1,3,2,0:T(8,128)(2,1)} %get-tuple-element.18) | copy-start | bytes 3145732
  344.7 4.7 %copy-start.1 = (bf16[1,128,768]{2,1,0:T(8,128)(2,1)S(1)}, bf16[1,128,768]{2,1,0:T(8,128)(2,1)}, u32[]{:S(2)}) copy-start(bf16[1,128,768]{2,1,0:T(8,128)(2,1)} %param.11) | copy-start | bytes 589828
Sparse Core Ops, SparseCore 0:
  10.4 71.8 all-gather.2
  104.0 91.2 reduce-scatter.2
  197.9 43.1 reduce-scatter.4
